TPU v7x, 128 devices: a whole 4x4x4 slice. The times are simulated.
128 devices in a mesh: group: 8 (over z, core), member: 16 (over x, y).
Axes of the slice: x: 4, y: 4, z: 4, core: 2. Of those that a mesh axis runs over, the one named last changes fastest.
Arguments:
- hidden: bfloat16 [12288, 2048], P('group'), may hold values from -6 to 6
- token_slab: int32 [12288, 1], P(('group', 'member')), may hold values from 0 to 127; in each aligned block of 96 rows (0 to 95, 96 to 191, ...) at most 2 rows name the same one
- token_row: int32 [12288], P(('group', 'member')), may hold values from 0 to 2047
- slab_owner: int32 [128], replicated, may hold values from 0 to 127, each once
- ple_table: bfloat16 [262144, 256], P(('group', 'member')), may hold values from -0.375 to 0.375
- norm_gains: float32 [1, 3, 2048], replicated, may hold values from 0.1 to 1.9
- w_gate: bfloat16 [1, 2048, 8192], P(None, None, 'member'), may hold values from -0.125 to 0.125
- w_up: bfloat16 [1, 2048, 8192], P(None, None, 'member'), may hold values from -0.125 to 0.125
- w_down: bfloat16 [1, 8192, 2048], P(None, 'member'), may hold values from -0.0625 to 0.0625
- ple_gate: bfloat16 [1, 2048, 256], P(None, None, 'member'), may hold values from -0.125 to 0.125
- ple_proj: bfloat16 [1, 256, 2048], P(None, 'member'), may hold values from -0.375 to 0.375
Outputs:
- hidden_out: bfloat16 [12288, 2048], P('group')
Inputs may be any that keep to these rules, and one draw needn't show every extreme that they name: Within the 96 tokens of one device (aligned blocks of token_slab), no slab is named by more than 2 tokens. Each number appears once: slab s is stored in rows slab_owner[s] * 2048 to slab_owner[s] * 2048 + 2047 of ple_table.
All inputs are finite; a program needn't handle non-finite values.
Results may differ from a plain program's by a relative error of at most 0.0061.
Values may be sent and summed in bfloat16 or wider, within the bound.
A program may use at most 128 MiB of HBM per device.

v0:
```python
import jax
import jax.numpy as jnp
from jax import lax
from jax.sharding import PartitionSpec as P

PLE = 256
epsilon = 1e-06


def in_blocks(x, dim, devices):
    shape = x.shape
    parts = x.reshape(*shape[:dim], devices, shape[dim] // devices, *shape[dim + 1 :])
    return jnp.moveaxis(parts, dim, 0)


def joined_along(parts, dim):
    shape = list(parts.shape[1:])
    shape[dim] *= parts.shape[0]
    return jnp.moveaxis(parts, 0, dim).reshape(shape)


def exchange_both(x, axis, axes, splits, concats):
    sizes = [lax.axis_size(a) for a in axes]
    parts = in_blocks(x, splits[0], sizes[0])
    parts = jnp.moveaxis(in_blocks(parts, splits[1] + 1, sizes[1]), 0, 1)
    inside = parts.shape[2:]
    parts = parts.reshape(-1, *inside)
    parts = lax.all_to_all(parts, axis, split_axis=0, concat_axis=0, tiled=True)
    parts = joined_along(parts.reshape(*sizes, *inside), concats[0] + 1)
    return joined_along(parts, concats[1])


def norm_rows(values, scales):
    return values * lax.rsqrt(jnp.mean(values * values, axis=-1, keepdims=True) + epsilon) * scales


def lookup_rows(wanted, ple_table):
    flat_ids = wanted.reshape(-1) - 1
    one_hot = (
        flat_ids[:, None] == jnp.arange(ple_table.shape[0], dtype=jnp.int32)[None, :]
    ).astype(jnp.bfloat16)
    served = jnp.dot(one_hot, ple_table, preferred_element_type=jnp.float32).astype(jnp.bfloat16)
    return served.reshape(wanted.shape + (ple_table.shape[1],))


def request_slots(slab_ids, token_row, slab_owner, devices, slots):
    target = slab_owner[slab_ids]
    order = jnp.arange(token_row.shape[0], dtype=jnp.int32)
    earlier = (target[None, :] == target[:, None]) & (order[None, :] < order[:, None])
    slot_of = jnp.sum(earlier.astype(jnp.int32), axis=1)
    hit_map = (target[:, None, None] == jnp.arange(devices, dtype=jnp.int32)[None, :, None]) & (
        slot_of[:, None, None] == jnp.arange(slots, dtype=jnp.int32)[None, None, :]
    )
    requests = jnp.sum(jnp.where(hit_map, token_row[:, None, None] + 1, 0), axis=0)
    return (hit_map, requests)


def pick_rows(hit_map, returned):
    return jnp.einsum(
        "tdc,dcw->tw", hit_map.astype(jnp.bfloat16), returned, preferred_element_type=jnp.float32
    ).astype(jnp.bfloat16)


def combine_branch(current, partial_value, scales):
    summed = lax.psum(partial_value, "member")
    return current + norm_rows(summed, scales)


def per_device(
    hidden,
    token_slab,
    token_row,
    slab_owner,
    ple_table,
    norm_gains,
    w_gate,
    w_up,
    w_down,
    ple_gate,
    ple_proj,
):
    members = lax.axis_size("member")
    devices = lax.axis_size("group") * members
    tokens_here = token_row.shape[0]
    slots = max(2, (2 * tokens_here + devices - 1) // devices)
    slab_ids = token_slab[:, 0]
    hit_map, requests = request_slots(slab_ids, token_row, slab_owner, devices, slots)
    grouped = requests.reshape(lax.axis_size("group"), members, slots)
    received = lax.all_to_all(
        lax.all_to_all(grouped, "group", split_axis=0, concat_axis=0, tiled=True),
        "member",
        split_axis=1,
        concat_axis=1,
        tiled=True,
    )
    served = lookup_rows(received, ple_table)
    returned = exchange_both(served, ("group", "member"), ("group", "member"), (0, 1), (0, 1))
    own_rows = pick_rows(hit_map, returned.reshape(devices, slots, ple_table.shape[1]))
    per_member = ple_gate.shape[2]
    layers = w_gate.shape[0]
    pieces = own_rows.reshape(tokens_here, layers, members, per_member)
    columns = lax.all_to_all(pieces, "member", split_axis=2, concat_axis=0, tiled=True)
    ple_part = columns.reshape(-1, layers, per_member).astype(jnp.float32) * PLE**0.5
    current = hidden.astype(jnp.float32)
    normed = norm_rows(current, norm_gains[0, 0]).astype(jnp.bfloat16)
    gate_part = jnp.dot(normed, w_gate[0], preferred_element_type=jnp.float32)
    up_part = jnp.dot(normed, w_up[0], preferred_element_type=jnp.float32)
    activated = (jax.nn.gelu(gate_part, approximate=True) * up_part).astype(jnp.bfloat16)
    mlp_out = jnp.dot(activated, w_down[0], preferred_element_type=jnp.float32)
    current = combine_branch(current, mlp_out, norm_gains[0, 1])
    current_b = current.astype(jnp.bfloat16)
    ple_gate_out = jnp.dot(current_b, ple_gate[0], preferred_element_type=jnp.float32)
    ple_act = (jax.nn.gelu(ple_gate_out, approximate=True) * ple_part[:, 0, :]).astype(jnp.bfloat16)
    ple_out = jnp.dot(ple_act, ple_proj[0], preferred_element_type=jnp.float32)
    current = combine_branch(current, ple_out, norm_gains[0, 2])
    return current.astype(jnp.bfloat16)


def solution(mesh):
    return jax.shard_map(
        per_device,
        mesh=mesh,
        in_specs=(
            P("group", None),
            P(("group", "member"), None),
            P(("group", "member")),
            P(),
            P(("group", "member"), None),
            P(),
            P(None, None, "member"),
            P(None, None, "member"),
            P(None, "member", None),
            P(None, None, "member"),
            P(None, "member", None),
        ),
        out_specs=P("group", None),
        check_vma=False,
    )
```

profile of v0, /device:TPU:1, one launch (start us, length us, event | category | flops | bytes accessed | tf_op | source)
XLA Modules:
  0.0 437.7 jit_solution(8497324638105972487)
XLA Ops:
  6.5 0.0 copy-start
  6.5 0.0 copy-start.7
  6.5 0.0 all-reduce.3.cloned.1.call-start
  6.5 0.0 copy-start.3
  6.5 4.2 fusion
  10.8 0.0 copy-done.7
  10.8 0.5 copy-done.3
  11.3 6.8 %fusion.17 = f32[1536,512]{1,0:T(8,128)} fusion(bf16[1,2048,512]{2,1,0:T(8,128)(2,1)} %param.17, bf16[1536,2048]{1,0:T(8,128)(2,1)S(1)} %copy-done.3, f32[2048]{0:T(1024)S(1)} %bitcast.58, f32[1536]{0:T(1024)S(1)} %add_rsqrt_fusion.2), kind=kOutput, calls=%fused_computation.25 | convolution fusion | flops 3233808384 | bytes 11548672 | tf_op jit(solution)/shard_map/dot_general | solution.py:106
  18.1 0.0 copy-done
  18.1 13.3 %fusion.14 = f32[1536,2048]{1,0:T(8,128)} fusion(bf16[1,512,2048]{2,1,0:T(8,128)(2,1)S(1)} %copy-done, f32[1536,512]{1,0:T(8,128)} %fusion.17, bf16[1,2048,512]{2,1,0:T(8,128)(2,1)} %param.18, bf16[1536,2048]{1,0:T(8,128)(2,1)} %param.11, f32[2048]{0:T(1024)S(1)} %bitcast.59, f32[1536]{0:T(1024)S(1)} %add_rsqrt_fusion.2), kind=kOutput, calls=%fused_computation.22 | convolution fusion | flops 6462898176 | bytes 26228736 | tf_op jit(solution)/shard_map/dot_general | solution.py:109
  31.4 0.0 copy-start.8
  31.4 0.0 all-reduce.3.cloned.1.call-update
  31.4 0.0 all-reduce.5.cloned.1.call-start
  31.5 0.6 copy-done.9
  32.1 0.0 copy-done.2
  32.1 1.2 gather_fusion
  33.3 0.2 convert_reduce_fusion
  33.5 0.0 copy-done.10
  33.5 0.1 iota_compare_fusion.5
  33.6 0.1 fusion.30
  33.7 0.1 reshape.110
  33.8 11.2 %all_to_all.24 = s32[8,16,2]{1,2,0:T(2,128)S(1)} all-to-all(s32[8,16,2]{1,2,0:T(2,128)S(1)} %copy.33), channel_id=1, replica_groups=mesh['group'=8,'member'=16] {'group'}, dimensions={0} | all-to-all | bytes 2048 | tf_op jit(solution)/shard_map/all_to_all | solution.py:90
  45.0 0.1 copy.34
  45.1 13.2 %all_to_all.25 = s32[8,16,2]{0,2,1:T(2,128)S(1)} all-to-all(s32[8,16,2]{0,2,1:T(2,128)S(1)} %copy.34), channel_id=1, replica_groups=mesh['group'=8,'member'=16] {'member'}, dimensions={1} | all-to-all | bytes 2048 | tf_op jit(solution)/shard_map/all_to_all | solution.py:89
  58.3 0.1 copy.35
  58.4 0.1 copy.36
  58.5 0.1 sub.7
  58.7 0.0 copy-done.8
  58.7 0.5 fusion.26
  59.2 0.1 reshape_transpose_transpose_reshape_reshape_reshape.3
  59.2 16.6 %all_to_all.26 = bf16[128,1,1,2,256]{4,3,2,1,0:T(2,128)(2,1)S(1)} all-to-all(bf16[128,1,1,2,256]{4,3,2,1,0:T(2,128)(2,1)S(1)} %bitcast.52), channel_id=1, replica_groups=mesh['group'=8,'member'=16] {'group','member'}, dimensions={0} | all-to-all | bytes 262144 | tf_op jit(solution)/shard_map/all_to_all | solution.py:28
  75.8 0.2 fusion.27
  76.1 0.1 copy.39
  76.2 10.0 %all_to_all.27 = bf16[96,1,16,16]{0,3,1,2:T(8,128)(2,1)S(1)} all-to-all(bf16[96,1,16,16]{0,3,1,2:T(8,128)(2,1)S(1)} %bitcast.54), channel_id=1, replica_groups=mesh['group'=8,'member'=16] {'member'}, dimensions={2} | all-to-all | bytes 98304 | tf_op jit(solution)/shard_map/all_to_all | solution.py:102
  86.2 0.1 mul.160
  86.3 0.0 copy-start.5
  86.3 0.0 copy-start.6
  86.4 129.4 %all-reduce.3.cloned.1.call-done = f32[1536,2048]{1,0:T(8,128)} async-done(((f32[1536,2048]{1,0:T(8,128)}), f32[1536,2048]{1,0:T(8,128)}) %all-reduce.3.cloned.1.call-update) | async-done | bytes 12582928 | tf_op jit(solution)/shard_map/psum | solution.py:65
  215.7 5.5 %multiply_reduce_fusion.1 = f32[1536]{0:T(1024)S(1)} fusion(f32[1536,2048]{1,0:T(8,128)} %all-reduce.3.cloned.1.call-done), kind=kLoop, calls=%fused_computation.9 | loop fusion | flops 6289920 | bytes 12589056 | tf_op jit(solution)/shard_map/reduce_sum | solution.py:34
  221.2 0.0 copy-done.5
  221.2 0.0 copy-done.6
  221.2 11.5 %fusion.47 = f32[1536,2048]{1,0:T(8,128)} fusion(f32[1536,16]{0,1:T(8,128)S(1)} %mul.160, f32[1536,2048]{1,0:T(8,128)} %all-reduce.3.cloned.1.call-done, bf16[1536,2048]{1,0:T(8,128)(2,1)} %param.11, f32[2048]{0:T(1024)S(1)} %bitcast.55, f32[1536]{0:T(1024)S(1)} %add_rsqrt_fusion.1, bf16[1,16,2048]{2,1,0:T(8,128)(2,1)S(1)} %copy-done.5, ...), kind=kOutput, calls=%fused_computation.47 | convolution fusion | flops 217300992 | bytes 31700992 | tf_op jit(solution)/shard_map/dot_general | solution.py:114
  232.8 0.0 all-reduce.5.cloned.1.call-update
  232.8 178.6 %all-reduce.5.cloned.1.call-done = f32[1536,2048]{1,0:T(8,128)} async-done(((f32[1536,2048]{1,0:T(8,128)}), f32[1536,2048]{1,0:T(8,128)}) %all-reduce.5.cloned.1.call-update) | async-done | bytes 12582928 | tf_op jit(solution)/shard_map/psum | solution.py:65
  411.4 5.6 %multiply_reduce_fusion = f32[1536]{0:T(1024)S(1)} fusion(f32[1536,2048]{1,0:T(8,128)} %all-reduce.5.cloned.1.call-done), kind=kLoop, calls=%fused_computation.8 | loop fusion | flops 6289920 | bytes 12589056 | tf_op jit(solution)/shard_map/reduce_sum | solution.py:34
  417.1 2.5 copy-done.4
  419.6 11.3 %add_convert_fusion = bf16[1536,2048]{1,0:T(8,128)(2,1)} fusion(f32[1536,2048]{1,0:T(8,128)S(1)} %copy-done.4, f32[1536,2048]{1,0:T(8,128)} %all-reduce.3.cloned.1.call-done, bf16[1536,2048]{1,0:T(8,128)(2,1)} %param.11, f32[2048]{0:T(1024)S(1)} %bitcast.57, f32[1536]{0:T(1024)S(1)} %add_rsqrt_fusion, f32[2048]{0:T(1024)S(1)} %bitcast.56, ...), kind=kLoop, calls=%fused_computation.7 | loop fusion | flops 25165824 | bytes 37777408 | tf_op jit(solution)/shard_map/convert_element_type | solution.py:116
  430.9 0.0 copy-done.1
  (18 shorter events, 0.1 us)
Async XLA Ops:
  6.5 11.6 %copy-start = (bf16[1,512,2048]{2,1,0:T(8,128)(2,1)S(1)}, bf16[1,512,2048]{2,1,0:T(8,128)(2,1)}, u32[]{:S(2)}) copy-start(bf16[1,512,2048]{2,1,0:T(8,128)(2,1)} %param.19) | copy-start | bytes 6291460
  6.5 4.3 copy-start.7
  6.5 209.2 %all-reduce.3.cloned.1.call-start = ((), (), s32[]{:S(2)}) async-start(), calls=%async_computation.4 | async-start | bytes 25165824 | tf_op jit(solution)/shard_map/psum | solution.py:65
  6.5 4.8 %copy-start.3 = (bf16[1536,2048]{1,0:T(8,128)(2,1)S(1)}, bf16[1536,2048]{1,0:T(8,128)(2,1)}, u32[]{:S(2)}) copy-start(bf16[1536,2048]{1,0:T(8,128)(2,1)} %param.11) | copy-start | bytes 18874372
  31.4 0.7 copy-start.9
  31.4 0.7 copy-start.2
  31.4 2.1 copy-start.10
  31.4 27.3 %copy-start.8 = (bf16[2048,256]{1,0:T(8,128)(2,1)S(1)}, bf16[2048,256]{1,0:T(8,128)(2,1)}, u32[]{:S(2)}) copy-start(bf16[2048,256]{1,0:T(8,128)(2,1)} %param.15) | copy-start | bytes 3145732
  31.4 380.0 %all-reduce.5.cloned.1.call-start = ((), (), s32[]{:S(2)}) async-start(), calls=%async_computation.5 | async-start | bytes 25165824 | tf_op jit(solution)/shard_map/psum | solution.py:65
  86.3 134.9 %copy-start.5 = (bf16[1,16,2048]{2,1,0:T(8,128)(2,1)S(1)}, bf16[1,16,2048]{2,1,0:T(8,128)(2,1)}, u32[]{:S(2)}) copy-start(bf16[1,16,2048]{2,1,0:T(8,128)(2,1)} %param.21) | copy-start | bytes 196612
  86.3 134.9 %copy-start.6 = (bf16[1,2048,16]{1,2,0:T(8,128)(2,1)S(1)}, bf16[1,2048,16]{1,2,0:T(8,128)(2,1)}, u32[]{:S(2)}) copy-start(bf16[1,2048,16]{1,2,0:T(8,128)(2,1)} %param.20) | copy-start | bytes 196612
  411.4 8.2 %copy-start.4 = (f32[1536,2048]{1,0:T(8,128)S(1)}, f32[1536,2048]{1,0:T(8,128)}, u32[]{:S(2)}) copy-start(f32[1536,2048]{1,0:T(8,128)} %all-reduce.5.cloned.1.call-done) | copy-start | bytes 37748740
  419.6 11.3 %copy-start.1 = (bf16[1,512,2048]{2,1,0:T(8,128)(2,1)S(1)}, bf16[1,512,2048]{2,1,0:T(8,128)(2,1)}, u32[]{:S(2)}) copy-start(bf16[1,512,2048]{2,1,0:T(8,128)(2,1)} %param.19) | copy-start | bytes 6291460
Sparse Core Ops, SparseCore 0:
  31.6 184.1 all-reduce.2
  232.9 178.4 all-reduce.4
where the time goes:
time: 438 us
  waiting for transfers between devices  308 us (70%)
  blocking collectives  51 us (12%)
  matrix products  32.3 us (7%)
  other arithmetic  27 us (6%)
  between operations  13.6 us (3%)
  local copies, waits for them, and re-layouts  5.69 us (1%)
    psum x2, waiting for transfers between devices, combine_branch(): summed = lax.psum(partial_value, 'member')  308 us
    all_to_all x1, blocking collectives, exchange_both(): parts = lax.all_to_all(parts, axis, split_axis=0, concat_axis=0, tiled=True)  16.6 us
    reduce_sum x3, other arithmetic, norm_rows(): jnp.mean(values * values, axis=-1, keepdims=True) + epsilon  15.3 us
    dot_general x1, matrix products, per_device(): mlp_out = jnp.dot(activated, w_down[0], preferred_element_type=jnp.float32)  13.3 us
    all_to_all x1, blocking collectives, per_device(): lax.all_to_all(lax.all_to_all(grouped, 'group', split_axis=0, concat_axis...  13.2 us
    dot_general x1, matrix products, per_device(): ple_out = jnp.dot(ple_act, ple_proj[0], preferred_element_type=jnp.float32)  11.5 us
    convert_element_type x1, other arithmetic, per_device(): return current.astype(jnp.bfloat16)  11.3 us
    all_to_all x1, blocking collectives, per_device(): lax.all_to_all(grouped, 'group', split_axis=0, concat_axis=0, tiled=True)  11.2 us
  transfers between devices with their start and end apart: 2, of which 2 were waited for; matrix products, arithmetic and copies ran while one was open for 1% of the time, Pallas kernels for 0%

commit v1 on v0

--- a/solution.py
+++ b/solution.py
@@ -62,7 +62,12 @@
 
 
 def combine_branch(current, partial_value, scales):
-    summed = lax.psum(partial_value, "member")
+    size_here = lax.axis_size("member")
+    summed = partial_value
+    for j0 in [idx for idx in (1, 2, 4, 8, 16) if idx < size_here]:
+        long_array = tuple(((tick, tick ^ j0) for tick in range(size_here)))
+        k_now = lax.ppermute(summed, "member", long_array)
+        summed = summed + k_now
     return current + norm_rows(summed, scales)
 
 

time: 438 us -> 2320 us (5.30)
  waiting for transfers between devices: 308 us -> 1880 us
  blocking collectives: 51 us -> 300 us
  other arithmetic: 27 us -> 86.9 us
    ppermute x0 -> x8, waiting for transfers between devices: none -> 1880 us  [combine_branch(): k_now = lax.ppermute(summed, 'member', long_array)]
    psum x2 -> x0, waiting for transfers between devices: 308 us -> none  [combine_branch(): summed = lax.psum(partial_value, 'member')]
    all_to_all x1, blocking collectives: 13.2 us -> 255 us  [per_device(): lax.all_to_all(lax.all_to_all(grouped, 'group', split_axis=0, concat_axis...]
    add x0 -> x6, other arithmetic: none -> 44.8 us  [combine_branch(): summed = summed + k_now]
  transfers between devices with their start and end apart: 2 -> 8, of which waited for: 2 -> 7; matrix products, arithmetic and copies ran while one was open for 1% -> 0% of each run, Pallas kernels for 0% -> 0%
where the time goes in v1:
time: 2320 us
  waiting for transfers between devices  1880 us (81%)
  blocking collectives  300 us (13%)
  other arithmetic  86.9 us (4%)
  matrix products  34.1 us (1%)
    ppermute x8, waiting for transfers between devices, combine_branch(): k_now = lax.ppermute(summed, 'member', long_array)  1880 us
    all_to_all x1, blocking collectives, per_device(): lax.all_to_all(lax.all_to_all(grouped, 'group', split_axis=0, concat_axis...  255 us
  transfers between devices with their start and end apart: 8, of which 7 were waited for; matrix products, arithmetic and copies ran while one was open for 0% of the time, Pallas kernels for 0%

profile of v1, /device:TPU:1, one launch (start us, length us, event | category | flops | bytes accessed | tf_op | source)
XLA Modules:
  0.0 2317.1 jit_solution(16277484750303687362)
XLA Ops:
  0.0 4.2 fusion
  4.2 0.7 fusion.68
  5.0 8.6 fusion.17
  13.5 13.3 fusion.14
  26.9 2.1 collective-permute-start
  29.0 269.9 %collective-permute-done = f32[1536,2048]{1,0:T(8,128)S(1)} collective-permute-done((f32[1536,2048]{1,0:T(8,128)}, f32[1536,2048]{1,0:T(8,128)S(1)}, u32[]{:S(2)}, u32[]{:S(2)}) %collective-permute-start) | collective-permute-done | bytes 12582944 | tf_op jit(solution)/shard_map/ppermute | solution.py:69
  298.9 6.0 add.96
  304.9 3.2 collective-permute-start.1
  308.2 269.0 %collective-permute-done.1 = f32[1536,2048]{1,0:T(8,128)} collective-permute-done((f32[1536,2048]{1,0:T(8,128)S(1)}, f32[1536,2048]{1,0:T(8,128)}, u32[]{:S(2)}, u32[]{:S(2)}) %collective-permute-start.1) | collective-permute-done | bytes 12582944 | tf_op jit(solution)/shard_map/ppermute | solution.py:69
  577.2 6.0 add.97
  583.3 1.2 collective-permute-start.2
  584.6 268.3 %collective-permute-done.2 = f32[1536,2048]{1,0:T(8,128)S(1)} collective-permute-done((f32[1536,2048]{1,0:T(8,128)S(1)}, f32[1536,2048]{1,0:T(8,128)S(1)}, u32[]{:S(2)}, u32[]{:S(2)}) %collective-permute-start.2) | collective-permute-done | bytes 12582944 | tf_op jit(solution)/shard_map/ppermute | solution.py:69
  852.9 5.4 add.98
  858.3 2.5 collective-permute-start.3
  860.9 1.2 gather_fusion
  862.1 0.2 convert_reduce_fusion
  862.3 0.1 iota_compare_fusion.5
  862.4 0.1 fusion.30
  862.5 0.1 reshape.110
  862.6 13.8 all_to_all.24
  876.4 0.1 copy.34
  876.5 254.6 %all_to_all.25 = s32[8,16,2]{0,2,1:T(2,128)S(1)} all-to-all(s32[8,16,2]{0,2,1:T(2,128)S(1)} %copy.34), channel_id=1, replica_groups=mesh['group'=8,'member'=16] {'member'}, dimensions={1} | all-to-all | bytes 2048 | tf_op jit(solution)/shard_map/all_to_all | solution.py:94
  1131.1 0.1 copy.35
  1131.2 0.1 copy.36
  1131.3 0.1 sub.7
  1131.5 0.5 fusion.26
  1132.0 0.1 reshape_transpose_transpose_reshape_reshape_reshape.3
  1132.0 22.3 all_to_all.26
  1154.4 0.2 fusion.27
  1154.6 0.1 copy.39
  1154.7 9.1 all_to_all.27
  1163.9 0.1 mul.160
  1164.0 13.8 multiply_reduce_fusion.1
  1177.9 11.5 fusion.47
  1189.4 0.3 collective-permute-start.4
  1189.6 269.5 %collective-permute-done.4 = f32[1536,2048]{1,0:T(8,128)S(1)} collective-permute-done((f32[1536,2048]{1,0:T(8,128)}, f32[1536,2048]{1,0:T(8,128)S(1)}, u32[]{:S(2)}, u32[]{:S(2)}) %collective-permute-start.4) | collective-permute-done | bytes 12582944 | tf_op jit(solution)/shard_map/ppermute | solution.py:69
  1459.2 6.0 add.109
  1465.2 1.2 collective-permute-start.5
  1466.4 269.2 %collective-permute-done.5 = f32[1536,2048]{1,0:T(8,128)} collective-permute-done((f32[1536,2048]{1,0:T(8,128)S(1)}, f32[1536,2048]{1,0:T(8,128)}, u32[]{:S(2)}, u32[]{:S(2)}) %collective-permute-start.5) | collective-permute-done | bytes 12582944 | tf_op jit(solution)/shard_map/ppermute | solution.py:69
  1735.6 6.0 add.110
  1741.7 0.3 collective-permute-start.6
  1742.0 4.1 copy-done.3
  1746.1 263.5 %collective-permute-done.6 = f32[1536,2048]{1,0:T(8,128)} collective-permute-done((f32[1536,2048]{1,0:T(8,128)S(1)}, f32[1536,2048]{1,0:T(8,128)}, u32[]{:S(2)}, u32[]{:S(2)}) %collective-permute-start.6) | collective-permute-done | bytes 12582944 | tf_op jit(solution)/shard_map/ppermute | solution.py:69
  2009.6 15.2 add.111
  2024.8 0.9 collective-permute-start.7
  2025.8 267.7 %collective-permute-done.7 = f32[1536,2048]{1,0:T(8,128)} collective-permute-done((f32[1536,2048]{1,0:T(8,128)}, f32[1536,2048]{1,0:T(8,128)}, u32[]{:S(2)}, u32[]{:S(2)}) %collective-permute-start.7) | collective-permute-done | bytes 12582944 | tf_op jit(solution)/shard_map/ppermute | solution.py:69
  2293.5 13.8 multiply_reduce_fusion
  2307.4 9.7 add_convert_fusion
  (42 shorter events, 0.2 us)
Async XLA Ops:
  0.0 13.5 copy-start
  26.9 272.0 %collective-permute-start = (f32[1536,2048]{1,0:T(8,128)}, f32[1536,2048]{1,0:T(8,128)S(1)}, u32[]{:S(2)}, u32[]{:S(2)}) collective-permute-start(f32[1536,2048]{1,0:T(8,128)} %fusion.14), channel_id=1, source_target_pairs={{0,1},{1,0},{2,3},{3,2},{4,5},{5,4},{6,7},{7,6},{8,9},{9,8},{10,11... | collective-permute-start | bytes 37748744 | tf_op jit(solution)/shard_map/ppermute | solution.py:69
  304.9 272.3 %collective-permute-start.1 = (f32[1536,2048]{1,0:T(8,128)S(1)}, f32[1536,2048]{1,0:T(8,128)}, u32[]{:S(2)}, u32[]{:S(2)}) collective-permute-start(f32[1536,2048]{1,0:T(8,128)S(1)} %add.96), channel_id=1, source_target_pairs={{0,2},{1,3},{2,0},{3,1},{4,6},{5,7},{6,4},{7,5},{8,10},{9,11},{10,... | collective-permute-start | bytes 37748744 | tf_op jit(solution)/shard_map/ppermute | solution.py:69
  583.3 277.6 %copy-start.7 = (s32[96,1]{0,1:T(1,128)S(1)}, s32[96,1]{0,1:T(1,128)}, u32[]{:S(2)}) copy-start(s32[96,1]{0,1:T(1,128)} %param.12) | copy-start | bytes 1156
  583.3 277.6 %copy-start.2 = (s32[128]{0:T(128)S(1)}, s32[128]{0:T(128)}, u32[]{:S(2)}) copy-start(s32[128]{0:T(128)} %param.14) | copy-start | bytes 1540
  583.3 279.0 %copy-start.8 = (s32[96]{0:T(128)S(1)}, s32[96]{0:T(128)}, u32[]{:S(2)}) copy-start(s32[96]{0:T(128)} %param.13) | copy-start | bytes 1156
  583.3 548.2 %copy-start.6 = (bf16[2048,256]{1,0:T(8,128)(2,1)S(1)}, bf16[2048,256]{1,0:T(8,128)(2,1)}, u32[]{:S(2)}) copy-start(bf16[2048,256]{1,0:T(8,128)(2,1)} %param.15) | copy-start | bytes 3145732
  583.3 269.6 %collective-permute-start.2 = (f32[1536,2048]{1,0:T(8,128)S(1)}, f32[1536,2048]{1,0:T(8,128)S(1)}, u32[]{:S(2)}, u32[]{:S(2)}) collective-permute-start(f32[1536,2048]{1,0:T(8,128)S(1)} %add.97), channel_id=1, source_target_pairs={{0,4},{1,5},{2,6},{3,7},{4,0},{5,1},{6,2},{7,3},{8,12},{9,13},{10,... | collective-permute-start | bytes 37748744 | tf_op jit(solution)/shard_map/ppermute | solution.py:69
  858.3 305.7 %collective-permute-start.3 = (f32[1536,2048]{1,0:T(8,128)}, f32[1536,2048]{1,0:T(8,128)}, u32[]{:S(2)}, u32[]{:S(2)}) collective-permute-start(f32[1536,2048]{1,0:T(8,128)} %add.98), channel_id=1, source_target_pairs={{0,8},{1,9},{2,10},{3,11},{4,12},{5,13},{6,14},{7,15},{8,0},{9,1},... | collective-permute-start | bytes 37748744 | tf_op jit(solution)/shard_map/ppermute | solution.py:69
  1164.0 13.9 copy-start.4
  1164.0 13.9 copy-start.5
  1189.4 269.8 %collective-permute-start.4 = (f32[1536,2048]{1,0:T(8,128)}, f32[1536,2048]{1,0:T(8,128)S(1)}, u32[]{:S(2)}, u32[]{:S(2)}) collective-permute-start(f32[1536,2048]{1,0:T(8,128)} %fusion.47), channel_id=1, source_target_pairs={{0,1},{1,0},{2,3},{3,2},{4,5},{5,4},{6,7},{7,6},{8,9},{9,8},{10,11... | collective-permute-start | bytes 37748744 | tf_op jit(solution)/shard_map/ppermute | solution.py:69
  1465.2 270.4 %collective-permute-start.5 = (f32[1536,2048]{1,0:T(8,128)S(1)}, f32[1536,2048]{1,0:T(8,128)}, u32[]{:S(2)}, u32[]{:S(2)}) collective-permute-start(f32[1536,2048]{1,0:T(8,128)S(1)} %add.109), channel_id=1, source_target_pairs={{0,2},{1,3},{2,0},{3,1},{4,6},{5,7},{6,4},{7,5},{8,10},{9,11},{10,... | collective-permute-start | bytes 37748744 | tf_op jit(solution)/shard_map/ppermute | solution.py:69
  1741.6 4.5 copy-start.3
  1741.7 267.9 %collective-permute-start.6 = (f32[1536,2048]{1,0:T(8,128)S(1)}, f32[1536,2048]{1,0:T(8,128)}, u32[]{:S(2)}, u32[]{:S(2)}) collective-permute-start(f32[1536,2048]{1,0:T(8,128)S(1)} %add.110), channel_id=1, source_target_pairs={{0,4},{1,5},{2,6},{3,7},{4,0},{5,1},{6,2},{7,3},{8,12},{9,13},{10,... | collective-permute-start | bytes 37748744 | tf_op jit(solution)/shard_map/ppermute | solution.py:69
  2009.6 297.7 %slice-start = ((s8[12582912]{0:T(1024)(128)(4,1)}), s8[4194304]{0:T(1024)(128)(4,1)S(1)}, s32[]{:S(2)}) async-start(s8[12582912]{0:T(1024)(128)(4,1)} %bitcast.51), calls=%async_computation.4 | async-start | bytes 8388608
  2009.6 297.7 %slice-start.1 = ((s8[12582912]{0:T(1024)(128)(4,1)}), s8[4194304]{0:T(1024)(128)(4,1)S(1)}, s32[]{:S(2)}) async-start(s8[12582912]{0:T(1024)(128)(4,1)} %bitcast.51), calls=%async_computation.5 | async-start | bytes 8388608
  2009.6 297.7 %slice-start.3 = ((s8[6291456]{0:T(1024)(128)(4,1)}), s8[4194304]{0:T(1024)(128)(4,1)S(1)}, s32[]{:S(2)}) async-start(s8[6291456]{0:T(1024)(128)(4,1)} %bitcast.53), calls=%async_computation.7 | async-start | bytes 8388608
  2024.8 282.5 %slice-start.2 = ((s8[12582912]{0:T(1024)(128)(4,1)}), s8[4194304]{0:T(1024)(128)(4,1)S(1)}, s32[]{:S(2)}) async-start(s8[12582912]{0:T(1024)(128)(4,1)} %bitcast.51), calls=%async_computation.6 | async-start | bytes 8388608
  2024.8 282.5 %slice-start.4 = ((s8[6291456]{0:T(1024)(128)(4,1)}), s8[2097152]{0:T(1024)(128)(4,1)S(1)}, s32[]{:S(2)}) async-start(s8[6291456]{0:T(1024)(128)(4,1)} %bitcast.53), calls=%async_computation.8 | async-start | bytes 4194304
  2024.8 268.7 %collective-permute-start.7 = (f32[1536,2048]{1,0:T(8,128)}, f32[1536,2048]{1,0:T(8,128)}, u32[]{:S(2)}, u32[]{:S(2)}) collective-permute-start(f32[1536,2048]{1,0:T(8,128)} %add.111), channel_id=1, source_target_pairs={{0,8},{1,9},{2,10},{3,11},{4,12},{5,13},{6,14},{7,15},{8,0},{9,1},... | collective-permute-start | bytes 37748744 | tf_op jit(solution)/shard_map/ppermute | solution.py:69
  2307.3 9.8 copy-start.1
